TPU v7x, 256 devices: a whole 4x4x8 slice. The times are simulated.
256 devices in a mesh: dp: 4 (over y), blocks: 64 (over x, z, core).
Axes of the slice: x: 4, y: 4, z: 8, core: 2. Of those that a mesh axis runs over, the one named last changes fastest.
Arguments:
- tokens: bfloat16 [16384, 8192], P('blocks', 'dp'), may hold values from -6 to 6
- dec_bias: float32 [8192], P('dp'), may hold values from -3 to 3
- routes: int32 [16384, 2], P('blocks'), may hold values from 0 to 63, all different within a row; in each aligned block of 256 rows (0 to 255, 256 to 511, ...) at most 16 rows name the same one
- latent_picks: int32 [16384, 2, 16], P('blocks'), may hold values from 0 to 1023
- enc_weight: bfloat16 [64, 8192, 1024], P('blocks', 'dp'), may hold values from -0.0625 to 0.0625
- dec_weight: bfloat16 [64, 1024, 8192], P('blocks', None, 'dp'), may hold values from -1 to 1
- enc_bias: float32 [64, 1024], P('blocks'), may hold values from -3 to 3
Outputs:
- reconstruction: bfloat16 [16384, 8192], P('blocks', 'dp')
Inputs may be any that keep to these rules, and one draw needn't show every extreme that they name: `routes`: each row names 2 different blocks; among the rows of one index of blocks no block is named by more than 16 rows, and some block by exactly 16. `latent_picks`: indices within a block; a row may name an index more than once.
All inputs are finite; a program needn't handle non-finite values.
Results may differ from a plain program's by a relative error of at most 0.0059.
Values may be sent and summed in bfloat16 or wider, within the bound.
A program may use at most 64 MiB of HBM per device.

v0:
```python
import jax
import jax.numpy as jnp
from jax import lax
from jax.sharding import PartitionSpec as P


def on_device(tokens, dec_bias, routes, latent_picks, enc_weight, dec_weight, enc_bias):
    tok_rows, quarter = tokens.shape
    top_blocks = routes.shape[1]
    pick_count = latent_picks.shape[2]
    latents = enc_weight.shape[2]
    blk_count = lax.axis_size("blocks")
    capacity = max(2, 2 * tok_rows * top_blocks // blk_count)
    slot_count = blk_count * capacity
    pair_count = tok_rows * top_blocks
    centered = (tokens.astype(jnp.float32) - dec_bias).astype(jnp.bfloat16)
    owners = routes.reshape(pair_count)
    onehot = (owners[:, None] == jnp.arange(blk_count, dtype=jnp.int32)[None, :]).astype(jnp.int32)
    slot_rank = jnp.sum(jnp.cumsum(onehot, axis=0) * onehot, axis=1) - 1
    target = owners * capacity + slot_rank
    placing = jnp.arange(slot_count, dtype=jnp.int32)[:, None] == target[None, :]
    place_half = placing.astype(jnp.bfloat16)
    paired = jnp.repeat(centered, top_blocks, axis=0)
    outgoing = jnp.dot(place_half, paired, preferred_element_type=jnp.float32).astype(jnp.bfloat16)
    outgoing = outgoing.reshape(blk_count, capacity, quarter)
    sent_picks = jnp.dot(
        placing.astype(jnp.float32),
        latent_picks.reshape(pair_count, pick_count).astype(jnp.float32),
        precision=lax.Precision.HIGHEST,
    ).astype(jnp.int32)
    sent_picks = sent_picks.reshape(blk_count, capacity, pick_count)
    enc_local = enc_weight[0]
    dec_local = dec_weight[0]
    bias_local = enc_bias[0]
    lat_ids = jnp.arange(latents, dtype=jnp.int32)
    arrived = lax.all_to_all(outgoing, "blocks", split_axis=0, concat_axis=0, tiled=True)
    chosen = lax.all_to_all(sent_picks, "blocks", split_axis=0, concat_axis=0, tiled=True)
    item_count = arrived.shape[1]
    flat_rows = arrived.reshape(blk_count * item_count, quarter)
    chosen_ids = chosen.reshape(blk_count * item_count, pick_count)
    partial_value = jnp.dot(flat_rows, enc_local, preferred_element_type=jnp.float32)
    summed = lax.psum(partial_value, "dp") + bias_local[None, :]
    keep_mask = jnp.any(chosen_ids[:, :, None] == lat_ids[None, None, :], axis=1)
    active = jnp.where(keep_mask, jnp.maximum(summed, 0.0), 0.0).astype(jnp.bfloat16)
    partial_out = jnp.dot(active, dec_local, preferred_element_type=jnp.float32).astype(
        jnp.bfloat16
    )
    partial_out = partial_out.reshape(blk_count, item_count, quarter)
    returned = lax.all_to_all(partial_out, "blocks", split_axis=0, concat_axis=0, tiled=True)
    back_rows = returned.reshape(slot_count, quarter)
    per_pair = jnp.einsum("sp,sd->pd", place_half, back_rows, preferred_element_type=jnp.float32)
    summed_out = per_pair.reshape(tok_rows, top_blocks, quarter).sum(axis=1) + dec_bias
    return summed_out.astype(jnp.bfloat16)


def solution(mesh):
    in_specs = (
        P("blocks", "dp"),
        P("dp"),
        P("blocks", None),
        P("blocks", None, None),
        P("blocks", "dp", None),
        P("blocks", None, "dp"),
        P("blocks", None),
    )
    out_specs = P("blocks", "dp")
    return jax.shard_map(
        on_device, mesh=mesh, in_specs=in_specs, out_specs=out_specs, check_vma=False
    )
```

profile of v0, /device:TPU:1, one launch (start us, length us, event | category | flops | bytes accessed | tf_op | source)
XLA Modules:
  0.0 357.7 jit_solution(9807614320305272181)
XLA Ops:
  6.5 0.0 all-reduce.2.cloned.1.call-start
  6.5 0.8 copy.23
  7.4 0.1 eq.70
  7.5 0.1 reshape.77
  7.7 1.2 reduce-window.6
  8.9 0.2 slice_reduce_fusion
  9.1 0.1 fusion.20
  9.3 1.5 subtract_convert_fusion
  10.8 1.3 broadcast_in_dim.3
  12.1 2.2 reshape.80
  14.3 3.9 %convolution_convert_fusion = bf16[1024,2048]{1,0:T(8,128)(2,1)S(1)} fusion(bf16[512,2048]{1,0:T(8,128)(2,1)} %reshape.80, s32[512]{0:T(512)S(1)} %add_add_fusion), kind=kOutput, calls=%fused_computation.7 | convolution fusion | flops 2150105088 | bytes 6293504 | tf_op jit(solution)/shard_map/dot_general | solution.py:24
  18.2 0.0 copy-start.2
  18.2 109.2 %all_to_all.15 = bf16[64,16,2048]{2,1,0:T(8,128)(2,1)S(1)} all-to-all(bf16[64,16,2048]{2,1,0:T(8,128)(2,1)S(1)} %bitcast.43), channel_id=1, replica_groups=mesh['dp'=4,'blocks'=64] {'blocks'}, dimensions={0} | all-to-all | bytes 8388608 | tf_op jit(solution)/shard_map/all_to_all | solution.py:36
  127.5 0.0 copy-done.2
  127.5 6.0 %fusion.3 = f32[1024,1024]{1,0:T(8,128)} fusion(bf16[1024,2048]{1,0:T(8,128)(2,1)S(1)} %bitcast.44, bf16[1,2048,1024]{2,1,0:T(8,128)(2,1)S(1)} %copy-done.2), kind=kOutput, calls=%fused_computation.4 | convolution fusion | flops 4294967296 | bytes 12582912 | tf_op jit(solution)/shard_map/dot_general | solution.py:41
  133.5 0.0 copy-start.1
  133.5 0.0 all-reduce.2.cloned.1.call-update
  133.6 0.7 copy-done.1
  134.3 0.0 copy-start.3
  134.3 0.1 copy.26
  134.4 1.0 fusion.16
  135.5 0.2 reshape.79
  135.7 0.3 copy.40
  136.0 0.2 reshape.87
  136.2 15.4 %all_to_all.16 = s32[64,1,256]{2,1,0:T(1,128)S(1)} all-to-all(s32[64,1,256]{2,1,0:T(1,128)S(1)} %reshape.87), channel_id=1, replica_groups=mesh['dp'=4,'blocks'=64] {'blocks'}, dimensions={0} | all-to-all | bytes 131072 | tf_op jit(solution)/shard_map/all_to_all | solution.py:37
  151.7 0.5 broadcast.47
  152.2 0.8 reduce.2
  153.0 0.2 reshape.88
  153.2 0.2 copy.31
  153.4 13.1 %fusion = pred[1024,1024]{1,0:T(8,128)(4,1)S(1)} fusion(s32[1024,16]{1,0:T(8,128)S(1)} %bitcast.45), kind=kLoop, calls=%fused_computation.1 | loop fusion | flops 32505856 | bytes 1114112 | tf_op jit(solution)/shard_map/reduce_or | solution.py:43
  166.5 61.8 %all-reduce.2.cloned.1.call-done = f32[1024,1024]{1,0:T(8,128)} async-done(((f32[1024,1024]{1,0:T(8,128)}), f32[1024,1024]{1,0:T(8,128)}) %all-reduce.2.cloned.1.call-update) | async-done | bytes 4194320 | tf_op jit(solution)/shard_map/psum | solution.py:42
  228.3 0.0 copy-done.3
  228.3 10.0 %fusion.5 = bf16[1024,2048]{1,0:T(8,128)(2,1)} fusion(bf16[1,1024,2048]{2,1,0:T(8,128)(2,1)} %param.12, pred[1024,1024]{1,0:T(8,128)(4,1)S(1)} %fusion, f32[1024,1024]{1,0:T(8,128)} %all-reduce.2.cloned.1.call-done, f32[1024]{0:T(1024)S(1)} %bitcast.49), kind=kOutput, calls=%fused_computation.8 | convolution fusion | flops 4301258752 | bytes 13635584 | tf_op jit(solution)/shard_map/dot_general | solution.py:45
  238.3 10.8 %all-to-all-start.2 = ((bf16[64,16,2048]{2,1,0:T(8,128)(2,1)}), bf16[64,16,2048]{2,1,0:T(8,128)(2,1)}, u32[]{:S(2)}, u32[]{:S(2)}) async-start(bf16[64,16,2048]{2,1,0:T(8,128)(2,1)} %bitcast.42), calls=%async_computation.2 | async-start | bytes 8388608 | tf_op jit(solution)/shard_map/all_to_all | solution.py:49
  249.1 0.4 iota_compare_fusion.4
  249.5 1.0 eq.76
  250.5 94.5 %all-to-all-done.2 = bf16[64,16,2048]{2,1,0:T(8,128)(2,1)} async-done(((bf16[64,16,2048]{2,1,0:T(8,128)(2,1)}), bf16[64,16,2048]{2,1,0:T(8,128)(2,1)}, u32[]{:S(2)}, u32[]{:S(2)}) %all-to-all-start.2) | async-done | bytes 4194336 | tf_op jit(solution)/shard_map/all_to_all | solution.py:49
  345.0 0.0 copy-start
  345.0 4.7 %fusion.13 = f32[256,2048]{1,0:T(8,128)S(1)} fusion(bf16[1024,2048,1]{1,0,2:T(8,128)(2,1)} %bitcast.10, pred[256,2,1024]{2,1,0:T(4,128)(4,1)S(1)} %eq.76), kind=kOutput, calls=%fused_computation.18 | convolution fusion | flops 2148007936 | bytes 6815744 | tf_op jit(solution)/shard_map/sp,sd->pd/dot_general | solution.py:51
  349.7 0.0 copy-done
  349.7 1.2 add_convert_fusion
  (5 shorter events, 0.1 us)
Async XLA Ops:
  6.5 221.8 %all-reduce.2.cloned.1.call-start = ((), (), s32[]{:S(2)}) async-start(), calls=%async_computation.3 | async-start | bytes 8388608 | tf_op jit(solution)/shard_map/psum | solution.py:42
  18.2 109.3 %copy-start.2 = (bf16[1,2048,1024]{2,1,0:T(8,128)(2,1)S(1)}, bf16[1,2048,1024]{2,1,0:T(8,128)(2,1)}, u32[]{:S(2)}) copy-start(bf16[1,2048,1024]{2,1,0:T(8,128)(2,1)} %param.11) | copy-start | bytes 12582916
  133.5 0.8 copy-start.1
  134.3 94.0 %copy-start.3 = (f32[1,1024]{1,0:T(1,128)S(1)}, f32[1,1024]{1,0:T(1,128)}, u32[]{:S(2)}) copy-start(f32[1,1024]{1,0:T(1,128)} %param.13) | copy-start | bytes 12292
  238.3 106.7 %all-to-all-start.2 = ((bf16[64,16,2048]{2,1,0:T(8,128)(2,1)}), bf16[64,16,2048]{2,1,0:T(8,128)(2,1)}, u32[]{:S(2)}, u32[]{:S(2)}) async-start(bf16[64,16,2048]{2,1,0:T(8,128)(2,1)} %bitcast.42), calls=%async_computation.2 | async-start | bytes 8388608 | tf_op jit(solution)/shard_map/all_to_all | solution.py:49
  345.0 4.7 %copy-start = (f32[2048]{0:T(1024)S(1)}, f32[2048]{0:T(1024)}, u32[]{:S(2)}) copy-start(f32[2048]{0:T(1024)} %param.8) | copy-start | bytes 24580
Sparse Core Ops, SparseCore 0:
  133.7 94.5 all-reduce.1
where the time goes:
time: 358 us
  waiting for transfers between devices  156 us (44%)
  blocking collectives  125 us (35%)
  matrix products  25.6 us (7%)
  other arithmetic  18.3 us (5%)
  between operations  13.6 us (4%)
  starting transfers between devices  10.8 us (3%)
  local copies, waits for them, and re-layouts  8.35 us (2%)
    all_to_all x1, blocking collectives, on_device(): lax.all_to_all(outgoing, 'blocks', split_axis=0, concat_axis=0, tiled=True)  109 us
    all_to_all x1, waiting for transfers between devices, on_device(): lax.all_to_all(partial_out, 'blocks', split_axis=0, concat_axis=0, tiled=...  94.5 us
    psum x1, waiting for transfers between devices, on_device(): summed = lax.psum(partial_value, 'dp') + bias_local[None, :]  61.8 us
    all_to_all x1, blocking collectives, on_device(): lax.all_to_all(sent_picks, 'blocks', split_axis=0, concat_axis=0, tiled=T...  15.4 us
    reduce_or x1, other arithmetic, on_device(): jnp.any(chosen_ids[:, :, None] == lat_ids[None, None, :], axis=1)  13.1 us
    all_to_all x1, starting transfers between devices, on_device(): lax.all_to_all(partial_out, 'blocks', split_axis=0, concat_axis=0, tiled=...  10.8 us
    dot_general x1, matrix products, on_device(): jnp.dot(active, dec_local, preferred_element_type=jnp.float32)  9.97 us
  transfers between devices with their start and end apart: 2, of which 2 were waited for; matrix products, arithmetic and copies ran while one was open for 5% of the time, Pallas kernels for 0%

commit v1 on v0

--- a/solution.py
+++ b/solution.py
@@ -39,7 +39,7 @@
     flat_rows = arrived.reshape(blk_count * item_count, quarter)
     chosen_ids = chosen.reshape(blk_count * item_count, pick_count)
     partial_value = jnp.dot(flat_rows, enc_local, preferred_element_type=jnp.float32)
-    summed = lax.psum(partial_value, "dp") + bias_local[None, :]
+    summed = jnp.sum(lax.all_gather(partial_value, "dp"), axis=0) + bias_local[None, :]
     keep_mask = jnp.any(chosen_ids[:, :, None] == lat_ids[None, None, :], axis=1)
     active = jnp.where(keep_mask, jnp.maximum(summed, 0.0), 0.0).astype(jnp.bfloat16)
     partial_out = jnp.dot(active, dec_local, preferred_element_type=jnp.float32).astype(

time: 358 us -> 427 us (1.19)
  waiting for transfers between devices: 156 us -> 215 us
  other arithmetic: 18.3 us -> 28.6 us
    all_gather x0 -> x1, waiting for transfers between devices: none -> 121 us  [on_device(): lax.all_gather(partial_value, 'dp')]
    psum x1 -> x0, waiting for transfers between devices: 61.8 us -> none  [on_device(): summed = lax.psum(partial_value, 'dp') + bias_local[None, :]]
    reduce_sum x0 -> x1, other arithmetic: none -> 10.3 us  [on_device(): jnp.sum(lax.all_gather(partial_value, 'dp'), axis=0) + bias_local[None, :]]
  transfers between devices with their start and end apart: 2 -> 2, of which waited for: 2 -> 2; matrix products, arithmetic and copies ran while one was open for 5% -> 4% of each run, Pallas kernels for 0% -> 0%
where the time goes in v1:
time: 427 us
  waiting for transfers between devices  215 us (50%)
  blocking collectives  125 us (29%)
  other arithmetic  28.6 us (7%)
  matrix products  25.5 us (6%)
  between operations  13.6 us (3%)
  starting transfers between devices  10.8 us (3%)
  local copies, waits for them, and re-layouts  8.35 us (2%)
    all_gather x1, waiting for transfers between devices, on_device(): lax.all_gather(partial_value, 'dp')  121 us
    all_to_all x1, blocking collectives, on_device(): lax.all_to_all(outgoing, 'blocks', split_axis=0, concat_axis=0, tiled=True)  109 us
    all_to_all x1, waiting for transfers between devices, on_device(): lax.all_to_all(partial_out, 'blocks', split_axis=0, concat_axis=0, tiled=...  94.5 us
    all_to_all x1, blocking collectives, on_device(): lax.all_to_all(sent_picks, 'blocks', split_axis=0, concat_axis=0, tiled=T...  15.4 us
    reduce_or x1, other arithmetic, on_device(): jnp.any(chosen_ids[:, :, None] == lat_ids[None, None, :], axis=1)  13.1 us
    all_to_all x1, starting transfers between devices, on_device(): lax.all_to_all(partial_out, 'blocks', split_axis=0, concat_axis=0, tiled=...  10.8 us
    reduce_sum x1, other arithmetic, on_device(): jnp.sum(lax.all_gather(partial_value, 'dp'), axis=0) + bias_local[None, :]  10.3 us
    dot_general x1, matrix products, on_device(): jnp.dot(active, dec_local, preferred_element_type=jnp.float32)  9.9 us
  transfers between devices with their start and end apart: 2, of which 2 were waited for; matrix products, arithmetic and copies ran while one was open for 4% of the time, Pallas kernels for 0%

profile of v1, /device:TPU:1, one launch (start us, length us, event | category | flops | bytes accessed | tf_op | source)
XLA Modules:
  0.0 426.6 jit_solution(12763269797102371363)
XLA Ops:
  6.5 0.0 all-gather.3.cloned.1.call-start
  6.5 0.8 copy.23
  7.4 0.1 eq.70
  7.5 0.1 reshape.77
  7.7 1.2 reduce-window.6
  8.9 0.2 slice_reduce_fusion
  9.1 0.1 fusion.20
  9.3 1.5 subtract_convert_fusion
  10.8 1.3 broadcast_in_dim.3
  12.1 2.2 reshape.80
  14.3 3.9 convolution_convert_fusion
  18.2 0.0 copy-start.2
  18.2 109.2 %all_to_all.15 = bf16[64,16,2048]{2,1,0:T(8,128)(2,1)S(1)} all-to-all(bf16[64,16,2048]{2,1,0:T(8,128)(2,1)S(1)} %bitcast.45), channel_id=1, replica_groups=mesh['dp'=4,'blocks'=64] {'blocks'}, dimensions={0} | all-to-all | bytes 8388608 | tf_op jit(solution)/shard_map/all_to_all | solution.py:36
  127.5 0.0 copy-done.2
  127.5 6.0 %fusion.3 = f32[1024,1024]{1,0:T(8,128)} fusion(bf16[1024,2048]{1,0:T(8,128)(2,1)S(1)} %bitcast.46, bf16[1,2048,1024]{2,1,0:T(8,128)(2,1)S(1)} %copy-done.2), kind=kOutput, calls=%fused_computation.4 | convolution fusion | flops 4294967296 | bytes 12582912 | tf_op jit(solution)/shard_map/dot_general | solution.py:41
  133.5 0.0 copy-start.1
  133.5 0.0 all-gather.3.cloned.1.call-update
  133.5 0.7 copy-done.1
  134.3 0.1 copy.26
  134.4 1.0 fusion.16
  135.5 0.2 reshape.79
  135.7 0.3 copy.40
  136.0 0.2 reshape.88
  136.2 15.4 %all_to_all.16 = s32[64,1,256]{2,1,0:T(1,128)S(1)} all-to-all(s32[64,1,256]{2,1,0:T(1,128)S(1)} %reshape.88), channel_id=1, replica_groups=mesh['dp'=4,'blocks'=64] {'blocks'}, dimensions={0} | all-to-all | bytes 131072 | tf_op jit(solution)/shard_map/all_to_all | solution.py:37
  151.6 0.5 broadcast.47
  152.1 0.8 reduce.2
  153.0 0.2 reshape.89
  153.2 0.2 copy.31
  153.4 13.1 %fusion = pred[1024,1024]{1,0:T(8,128)(4,1)S(1)} fusion(s32[1024,16]{1,0:T(8,128)S(1)} %bitcast.47), kind=kLoop, calls=%fused_computation.1 | loop fusion | flops 32505856 | bytes 1114112 | tf_op jit(solution)/shard_map/reduce_or | solution.py:43
  166.5 120.5 %all-gather.3.cloned.1.call-done = f32[4096,1024]{1,0:T(8,128)} async-done(((f32[1024,1024]{1,0:T(8,128)}), f32[4096,1024]{1,0:T(8,128)}) %all-gather.3.cloned.1.call-update) | async-done | bytes 16777232 | tf_op jit(solution)/shard_map/all_gather | solution.py:42
  287.0 0.0 copy-start.3
  287.0 10.3 %reduce_sum.28 = f32[1024,1024]{1,0:T(8,128)} reduce(f32[4,1024,1024]{2,1,0:T(8,128)} %bitcast.43, f32[]{:T(128)} %constant.15.clone.1), dimensions={0}, to_apply=%region_4.5 | reduce | flops 3145728 | bytes 20971524 | tf_op jit(solution)/shard_map/reduce_sum | solution.py:42
  297.3 0.0 copy-done.3
  297.3 9.9 %fusion.5 = bf16[1024,2048]{1,0:T(8,128)(2,1)} fusion(bf16[1,1024,2048]{2,1,0:T(8,128)(2,1)} %param.12, pred[1024,1024]{1,0:T(8,128)(4,1)S(1)} %fusion, f32[1024,1024]{1,0:T(8,128)} %reduce_sum.28, f32[1024]{0:T(1024)S(1)} %bitcast.51), kind=kOutput, calls=%fused_computation.8 | convolution fusion | flops 4301258752 | bytes 13635584 | tf_op jit(solution)/shard_map/dot_general | solution.py:45
  307.2 10.8 %all-to-all-start.2 = ((bf16[64,16,2048]{2,1,0:T(8,128)(2,1)}), bf16[64,16,2048]{2,1,0:T(8,128)(2,1)}, u32[]{:S(2)}, u32[]{:S(2)}) async-start(bf16[64,16,2048]{2,1,0:T(8,128)(2,1)} %bitcast.44), calls=%async_computation.2 | async-start | bytes 8388608 | tf_op jit(solution)/shard_map/all_to_all | solution.py:49
  318.0 0.4 iota_compare_fusion.4
  318.4 1.0 eq.76
  319.4 94.5 %all-to-all-done.2 = bf16[64,16,2048]{2,1,0:T(8,128)(2,1)} async-done(((bf16[64,16,2048]{2,1,0:T(8,128)(2,1)}), bf16[64,16,2048]{2,1,0:T(8,128)(2,1)}, u32[]{:S(2)}, u32[]{:S(2)}) %all-to-all-start.2) | async-done | bytes 4194336 | tf_op jit(solution)/shard_map/all_to_all | solution.py:49
  413.9 0.0 copy-start
  413.9 4.7 %fusion.13 = f32[256,2048]{1,0:T(8,128)S(1)} fusion(bf16[1024,2048,1]{1,0,2:T(8,128)(2,1)} %bitcast.11, pred[256,2,1024]{2,1,0:T(4,128)(4,1)S(1)} %eq.76), kind=kOutput, calls=%fused_computation.18 | convolution fusion | flops 2148007936 | bytes 6815744 | tf_op jit(solution)/shard_map/sp,sd->pd/dot_general | solution.py:51
  418.6 0.0 copy-done
  418.6 1.2 add_convert_fusion
  (5 shorter events, 0.1 us)
Async XLA Ops:
  6.5 280.4 %all-gather.3.cloned.1.call-start = ((), (), s32[]{:S(2)}) async-start(), calls=%async_computation.3 | async-start | bytes 20971520 | tf_op jit(solution)/shard_map/all_gather | solution.py:42
  18.2 109.3 %copy-start.2 = (bf16[1,2048,1024]{2,1,0:T(8,128)(2,1)S(1)}, bf16[1,2048,1024]{2,1,0:T(8,128)(2,1)}, u32[]{:S(2)}) copy-start(bf16[1,2048,1024]{2,1,0:T(8,128)(2,1)} %param.11) | copy-start | bytes 12582916
  133.5 0.8 copy-start.1
  287.0 10.3 %copy-start.3 = (f32[1,1024]{1,0:T(1,128)S(1)}, f32[1,1024]{1,0:T(1,128)}, u32[]{:S(2)}) copy-start(f32[1,1024]{1,0:T(1,128)} %param.13) | copy-start | bytes 12292
  307.2 106.7 %all-to-all-start.2 = ((bf16[64,16,2048]{2,1,0:T(8,128)(2,1)}), bf16[64,16,2048]{2,1,0:T(8,128)(2,1)}, u32[]{:S(2)}, u32[]{:S(2)}) async-start(bf16[64,16,2048]{2,1,0:T(8,128)(2,1)} %bitcast.44), calls=%async_computation.2 | async-start | bytes 8388608 | tf_op jit(solution)/shard_map/all_to_all | solution.py:49
  413.9 4.7 %copy-start = (f32[2048]{0:T(1024)S(1)}, f32[2048]{0:T(1024)}, u32[]{:S(2)}) copy-start(f32[2048]{0:T(1024)} %param.8) | copy-start | bytes 24580
Sparse Core Ops, SparseCore 0:
  133.7 153.2 all-gather.2
